TPU v7x, 128 devices: a whole 4x4x4 slice. The times are simulated.
128 devices in a mesh: ang: 8 (over x, core), det: 16 (over z, y).
Axes of the slice: x: 4, y: 4, z: 4, core: 2. Of those that a mesh axis runs over, the one named last changes fastest.
Arguments:
- raw_counts: float32 [256, 128, 4096], P('ang', None, 'det'), may hold values from 0.15 to 0.9
- dark_field: float32 [128, 4096], P(None, 'det'), may hold values from 0 to 0.1
- flat_field: float32 [128, 4096], P(None, 'det'), may hold values from 0.8 to 1.2
- destinations: int32 [32, 1], replicated, may hold values from 0 to 15; in each aligned block of 32 rows (0 to 31, 32 to 63, ...) at most 4 rows name the same one
- band_offsets: int32 [4096], replicated, may hold values from 0 to 4092, as said below
- band_weights: float32 [4, 4096], replicated, may hold values from 0.05 to 0.5
Outputs:
- parallel_slabs: float32 [256, 64, 4, 4096], P('ang', 'det')
Inputs may be any that keep to these rules, and one draw needn't show every extreme that they name: `destinations`: no z-slab owner receives more than 4 row blocks, and some owner receives exactly 4. band_offsets[t] lies between t - 8 and t + 5.
All inputs are finite; a program needn't handle non-finite values.
Results may differ from a plain program's by a relative error of at most 0.0001.
Values sent between devices are 32-bit elements; how exact they have to be, the bound alone decides.
A program may use at most 64 MiB of HBM per device.

v0:
```python
import jax
import jax.numpy as jnp
from jax import lax
from jax.sharding import PartitionSpec as P

RB = 4
SMW = 4
ITERS = 3
HB = 8
BW = 4
MOST = 4


cauchy_scale = 0.2


def with_halo(x, sides, width):
    for axis, dim in sides:
        count, length = (lax.axis_size(axis), x.shape[dim])
        up = [(i, (i + 1) % count) for i in range(count - 1)]
        down = [(j, i) for i, j in up]
        last = lax.slice_in_dim(x, length - width, length, axis=dim)
        leading = lax.slice_in_dim(x, 0, width, axis=dim)
        before = lax.ppermute(last, axis, up)
        after = lax.ppermute(leading, axis, down)
        x = jnp.concatenate([before, x, after], axis=dim)
    return x


def smooth_local(values, first_col, total_cols):
    col_width = values.shape[2]
    padded = with_halo(values, (("det", 2),), SMW)
    summed = padded[:, :, 0:col_width]
    for position in range(1, 2 * SMW + 1):
        summed = summed + padded[:, :, position : position + col_width]
    columns = first_col + jnp.arange(col_width, dtype=jnp.int32)
    counts = jnp.minimum(columns + SMW, total_cols - 1) - jnp.maximum(columns - SMW, 0) + 1
    return summed / counts.astype(jnp.float32)


def band_sum(widened, relative, weights, col_width):
    summed = None
    for shift in range(-HB, HB + 1):
        coeff = jnp.zeros((col_width,), jnp.float32)
        for position in range(BW):
            coeff = coeff + jnp.where(relative == shift - position, weights[position], 0.0)
        term = coeff * widened[..., HB + shift : HB + shift + col_width]
        summed = term if summed is None else summed + term
    return summed


def slot_tables(destinations, owners, most):
    targets = destinations[:, 0]
    block_ids = jnp.arange(targets.shape[0], dtype=jnp.int32)
    same_earlier = (targets[:, None] == targets[None, :]) & (
        block_ids[None, :] < block_ids[:, None]
    )
    slot_rank = jnp.sum(same_earlier.astype(jnp.int32), axis=1)
    owner_ids = jnp.arange(owners, dtype=jnp.int32)
    rank_ids = jnp.arange(most, dtype=jnp.int32)
    matching = (
        (targets[None, None, :] == owner_ids[:, None, None])
        & (slot_rank[None, None, :] == rank_ids[None, :, None])
    ).astype(jnp.int32)
    chosen = jnp.sum(matching * block_ids[None, None, :], axis=2)
    filled = jnp.sum(matching, axis=2)
    return (chosen, filled)


def slot_blocks(values, destinations, owners):
    ang_dev, row_count, col_width = values.shape
    blocks = values.reshape(ang_dev, row_count // RB, RB, col_width)
    chosen, filled = slot_tables(destinations, owners, MOST)
    picked = jnp.take(blocks, chosen.reshape(-1), axis=1).reshape(
        ang_dev, owners, MOST, RB, col_width
    )
    return picked * filled[None, :, :, None, None].astype(jnp.float32)


def body(raw_counts, dark_field, flat_field, destinations, band_offsets, band_weights):
    ang_dev, row_count, col_width = raw_counts.shape
    owners = lax.axis_size("det")
    first_col = lax.axis_index("det") * col_width
    total_cols = col_width * owners
    angles = ang_dev * lax.axis_size("ang")
    projected = -jnp.log((raw_counts - dark_field) / (flat_field - dark_field))
    detail = projected - smooth_local(projected, first_col, total_cols)
    gain_map = lax.psum(jnp.sum(detail, axis=0), "ang") / angles
    for reweight_pass in range(ITERS):
        scaled = (detail - gain_map) / cauchy_scale
        weights = 1.0 / (1.0 + scaled * scaled)
        weighted = jnp.sum(weights * detail, axis=0)
        weight_total = jnp.sum(weights, axis=0)
        total_all, weighted_all = lax.psum((weight_total, weighted), "ang")
        gain_map = weighted_all / total_all
    corrected = projected - gain_map
    picked = slot_blocks(corrected, destinations, owners)
    relative_all = band_offsets - jnp.arange(total_cols, dtype=jnp.int32)
    arrived = lax.all_to_all(picked, "det", split_axis=1, concat_axis=4, tiled=True)
    pad_widths = [(0, 0)] * (arrived.ndim - 1) + [(HB, HB)]
    widened_all = jnp.pad(arrived, pad_widths)
    moved = band_sum(widened_all, relative_all, band_weights, arrived.shape[-1])
    return moved.reshape(ang_dev, MOST, RB, total_cols)


def solution(mesh):
    placed = (P("ang", None, "det"), P(None, "det"), P(None, "det"), P(), P(), P())
    return jax.shard_map(
        body, mesh=mesh, in_specs=placed, out_specs=P("ang", "det", None, None), check_vma=False
    )
```

profile of v0, /device:TPU:0, one launch (start us, length us, event | category | flops | bytes accessed | tf_op | source)
XLA Modules:
  0.0 520.7 jit_solution(13446992526522736455)
XLA Ops:
  6.5 5.5 %copy.19 = f32[32,128,256]{1,0,2:T(8,128)} copy(f32[32,128,256]{2,1,0:T(8,128)} %param.6) | data formatting | bytes 8388608 | tf_op args[0]
  12.3 3.0 log_negate_fusion
  15.3 2.0 copy-done
  17.3 3.6 collective-permute-start
  20.9 1.3 collective-permute-start.1
  22.8 4.3 collective-permute-done.1
  27.0 19.3 %fusion.36 = (f32[128,256]{0,1:T(8,128)}, f32[32,128,256]{1,0,2:T(8,128)}) fusion(f32[32,128,256]{1,0,2:T(8,128)} %copy-done, f32[256]{0:T(256)S(1)} %add_convert_fusion, f32[32,128,4]{1,0,2:T(8,128)S(1)} %collective-permute-done.1, f32[32,128,4]{1,0,2:T(8,128)S(1)} %collective-permute-done), kind=kLoop, calls=%fused_computation.112 | loop fusion | flops 19890176 | bytes 8651776 | tf_op jit(solution)/shard_map/reduce_sum | solution.py:88
  46.6 63.6 %all-reduce.9.cloned.1.call-done = f32[128,256]{0,1:T(8,128)} async-done(((f32[128,256]{0,1:T(8,128)}), f32[128,256]{0,1:T(8,128)}) %all-reduce.9.cloned.1.call-update) | async-done | bytes 131088 | tf_op jit(solution)/shard_map/psum | solution.py:88
  111.1 4.8 fusion.29
  116.4 59.1 %all-reduce.15.cloned.1.call-done = (f32[128,256]{0,1:T(8,128)}, f32[128,256]{0,1:T(8,128)}) async-done(((f32[128,256]{0,1:T(8,128)}, f32[128,256]{0,1:T(8,128)}), (f32[128,256]{0,1:T(8,128)}, f32[128,256]{0,1:T(8,128)})) %all-reduce.15.cloned.1.call-update) | async-done | bytes 262160 | tf_op jit(solution)/shard_map/psum | solution.py:94
  175.5 1.0 div.57
  176.5 4.8 fusion.30
  181.6 59.4 %all-reduce.13.cloned.1.call-done = (f32[128,256]{0,1:T(8,128)}, f32[128,256]{0,1:T(8,128)}) async-done(((f32[128,256]{0,1:T(8,128)}, f32[128,256]{0,1:T(8,128)}), (f32[128,256]{0,1:T(8,128)}, f32[128,256]{0,1:T(8,128)})) %all-reduce.13.cloned.1.call-update) | async-done | bytes 262160 | tf_op jit(solution)/shard_map/psum | solution.py:94
  242.0 4.8 fusion.31
  247.0 59.5 %all-reduce.11.cloned.1.call-done = (f32[128,256]{0,1:T(8,128)}, f32[128,256]{0,1:T(8,128)}) async-done(((f32[128,256]{0,1:T(8,128)}, f32[128,256]{0,1:T(8,128)}), (f32[128,256]{0,1:T(8,128)}, f32[128,256]{0,1:T(8,128)})) %all-reduce.11.cloned.1.call-update) | async-done | bytes 262160 | tf_op jit(solution)/shard_map/psum | solution.py:94
  307.5 5.4 %broadcast_subtract_fusion = f32[32,128,256]{1,0,2:T(8,128)} fusion(f32[128,256]{0,1:T(8,128)S(1)} %div.63, f32[128,256]{0,1:T(8,128)S(1)} %copy.20, f32[32,128,256]{1,0,2:T(8,128)} %copy.19, f32[128,256]{0,1:T(8,128)S(1)} %copy.18), kind=kLoop, calls=%fused_computation.59 | loop fusion | flops 4194304 | bytes 8781824 | tf_op jit(solution)/shard_map/sub | solution.py:96
  312.9 5.6 %copy.21 = f32[32,128,256]{2,0,1:T(8,128)} copy(f32[32,128,256]{1,0,2:T(8,128)} %broadcast_subtract_fusion) | data formatting | bytes 8388608 | tf_op jit(solution)/shard_map/sub | solution.py:96
  318.5 6.7 %gather_fusion = f32[64,32,4,256]{3,1,2,0:T(8,128)} fusion(f32[32,32,4,256]{3,0,2,1:T(8,128)} %bitcast.18, s32[1024]{0:T(1024)S(1)} %pad_clamp_fusion), kind=kCustom, calls=%fused_computation | custom fusion | bytes 16777472 | tf_op jit(solution)/shard_map/jit(_take)/gather | solution.py:74
  325.2 8.9 %select_multiply_fusion = f32[32,16,4,4,256]{4,0,3,2,1:T(8,128)} fusion(f32[32,16,4,4,256]{4,0,3,2,1:T(8,128)} %bitcast.20, f32[16,4]{1,0:T(8,128)S(1)} %copy.23, pred[16,4]{1,0:T(8,128)(4,1)S(1)} %copy.17), kind=kLoop, calls=%fused_computation.22 | loop fusion | flops 4194304 | bytes 16777536 | tf_op jit(solution)/shard_map/mul | solution.py:77
  334.0 7.2 %all-to-all-start = ((f32[32,16,4,4,256]{4,0,3,2,1:T(8,128)}), f32[32,16,4,4,256]{4,0,3,2,1:T(8,128)}, u32[]{:S(2)}, u32[]{:S(2)}) async-start(f32[32,16,4,4,256]{4,0,3,2,1:T(8,128)} %select_multiply_fusion), calls=%async_computation | async-start | bytes 16777216 | tf_op jit(solution)/shard_map/all_to_all | solution.py:99
  341.4 119.7 %all-to-all-done = f32[32,16,4,4,256]{4,0,3,2,1:T(8,128)} async-done(((f32[32,16,4,4,256]{4,0,3,2,1:T(8,128)}), f32[32,16,4,4,256]{4,0,3,2,1:T(8,128)}, u32[]{:S(2)}, u32[]{:S(2)}) %all-to-all-start) | async-done | bytes 8388640 | tf_op jit(solution)/shard_map/all_to_all | solution.py:99
  461.0 4.6 copy.26
  465.7 36.4 %add_bitcast_fusion = f32[32,4,4,4096]{3,0,2,1:T(8,128)} fusion(f32[32,1,4,4,4096]{4,0,3,2,1:T(8,128)S(1)} %bitcast.19, f32[4096]{0:T(1024)S(1)} %get-tuple-element.24, f32[4096]{0:T(1024)S(1)} %get-tuple-element.25, f32[4096]{0:T(1024)S(1)} %get-tuple-element.26, f32[4096]{0:T(1024)S(1)} %get-tuple-element.27, f32[4096]{0:T(1024)S(1)} %get-tuple-element.28, ...), kind=kLoop, calls=%fused_computation.1 | loop fusion | flops 69206016 | bytes 17055744 | tf_op jit(solution)/shard_map/reshape | solution.py:103
  502.0 12.2 %copy.25 = f32[32,4,4,4096]{3,2,1,0:T(4,128)} copy(f32[32,4,4,4096]{3,0,2,1:T(8,128)} %add_bitcast_fusion) | data formatting | bytes 16777216 | tf_op jit(solution)/shard_map/reshape | solution.py:103
  (42 shorter events, 5.0 us)
Async XLA Ops:
  6.5 5.5 %copy-start.1 = (f32[128,256]{1,0:T(8,128)S(1)}, f32[128,256]{1,0:T(8,128)}, u32[]{:S(2)}) copy-start(f32[128,256]{1,0:T(8,128)} %param.7) | copy-start | bytes 393220
  6.5 5.6 %copy-start.2 = (f32[128,256]{1,0:T(8,128)S(1)}, f32[128,256]{1,0:T(8,128)}, u32[]{:S(2)}) copy-start(f32[128,256]{1,0:T(8,128)} %param.8) | copy-start | bytes 393220
  6.5 103.7 %all-reduce.9.cloned.1.call-start = ((), (), s32[]{:S(2)}) async-start(), calls=%async_computation.1 | async-start | bytes 262144 | tf_op jit(solution)/shard_map/psum | solution.py:88
  12.2 9.9 %copy-start.5 = (s32[32,1]{0,1:T(1,128)S(1)}, s32[32,1]{0,1:T(1,128)}, u32[]{:S(2)}) copy-start(s32[32,1]{0,1:T(1,128)} %param.9) | copy-start | bytes 388
  15.3 2.0 copy-start
  17.3 5.5 %collective-permute-start = (f32[32,128,4]{1,0,2:T(8,128)S(1)}, f32[32,128,4]{1,0,2:T(8,128)S(1)}, u32[]{:S(2)}, u32[]{:S(2)}) collective-permute-start(f32[32,128,4]{1,0,2:T(8,128)S(1)} %get-tuple-element.21), channel_id=1, source_target_pairs={{0,1},{1,2},{2,3},{3,4},{4,5},{5,6},{6,7},{7,8},{8,9},{9,10},{10,1... | collective-permute-start | bytes 196616 | tf_op jit(solution)/shard_map/ppermute | solution.py:24
  20.9 6.2 %collective-permute-start.1 = (f32[32,128,4]{1,0,2:T(8,128)S(1)}, f32[32,128,4]{1,0,2:T(8,128)S(1)}, u32[]{:S(2)}, u32[]{:S(2)}) collective-permute-start(f32[32,128,4]{1,0,2:T(8,128)S(1)} %get-tuple-element.22), channel_id=1, source_target_pairs={{1,0},{2,1},{3,2},{4,3},{5,4},{6,5},{7,6},{8,7},{9,8},{10,9},{11,1... | collective-permute-start | bytes 196616 | tf_op jit(solution)/shard_map/ppermute | solution.py:25
  46.3 129.2 %all-reduce.15.cloned.1.call-start = ((), (), s32[]{:S(2)}) async-start(), calls=%async_computation.4 | async-start | bytes 524288 | tf_op jit(solution)/shard_map/psum | solution.py:94
  116.0 125.0 %all-reduce.13.cloned.1.call-start = ((), (), s32[]{:S(2)}) async-start(), calls=%async_computation.3 | async-start | bytes 524288 | tf_op jit(solution)/shard_map/psum | solution.py:94
  181.4 125.1 %all-reduce.11.cloned.1.call-start = ((), (), s32[]{:S(2)}) async-start(), calls=%async_computation.2 | async-start | bytes 524288 | tf_op jit(solution)/shard_map/psum | solution.py:94
  334.0 7.2 %copy-start.3 = (f32[4,4096]{1,0:T(4,128)S(1)}, f32[4,4096]{1,0:T(4,128)}, u32[]{:S(2)}) copy-start(f32[4,4096]{1,0:T(4,128)} %param.11) | copy-start | bytes 196612
  334.0 7.3 %copy-start.4 = (s32[4096]{0:T(1024)S(1)}, s32[4096]{0:T(1024)}, u32[]{:S(2)}) copy-start(s32[4096]{0:T(1024)} %param.10) | copy-start | bytes 49156
  334.0 127.0 %all-to-all-start = ((f32[32,16,4,4,256]{4,0,3,2,1:T(8,128)}), f32[32,16,4,4,256]{4,0,3,2,1:T(8,128)}, u32[]{:S(2)}, u32[]{:S(2)}) async-start(f32[32,16,4,4,256]{4,0,3,2,1:T(8,128)} %select_multiply_fusion), calls=%async_computation | async-start | bytes 16777216 | tf_op jit(solution)/shard_map/all_to_all | solution.py:99
Sparse Core Ops, SparseCore 0:
  46.5 63.7 all-reduce.8
  116.1 59.3 all-reduce.14
  181.5 59.4 all-reduce.12
  246.9 59.5 all-reduce.10
where the time goes:
time: 527 us; the launch traced here: 521 us
  waiting for transfers between devices  366 us (69%)
  other arithmetic  91.8 us (17%)
  local copies, waits for them, and re-layouts  37.1 us (7%)
  between operations  13.3 us (3%)
  starting transfers between devices  12.4 us (2%)
    psum x3, waiting for transfers between devices, body(): total_all, weighted_all = lax.psum((weight_total, weighted), 'ang')  178 us
    all_to_all x1, waiting for transfers between devices, body(): lax.all_to_all(picked, 'det', split_axis=1, concat_axis=4, tiled=True)  120 us
    psum x1, waiting for transfers between devices, body(): gain_map = lax.psum(jnp.sum(detail, axis=0), 'ang') / angles  63.6 us
    reshape x1, other arithmetic, body(): return moved.reshape(ang_dev, MOST, RB, total_cols)  36.4 us
    reduce_sum x1, other arithmetic, body(): gain_map = lax.psum(jnp.sum(detail, axis=0), 'ang') / angles  19.3 us
    reduce_sum x3, other arithmetic, body(): weight_total = jnp.sum(weights, axis=0)  14.4 us
    reshape x1, local copies, waits for them, and re-layouts, body(): return moved.reshape(ang_dev, MOST, RB, total_cols)  12.2 us
  transfers between devices with their start and end apart: 7, of which 7 were waited for; matrix products, arithmetic and copies ran while one was open for 0% of the time, Pallas kernels for 0%

commit v1 on v0

v1 whole, which is shorter than its diff:
```python
import functools

import jax
import jax.numpy as jnp
from jax import lax
from jax.experimental import pallas as pl
from jax.experimental.pallas import tpu as pltpu
from jax.sharding import PartitionSpec as P

RB = 4
SMW = 4
ITERS = 3
BW = 4
MOST = 4
NBLK = 32
NDET = 16
SIDE = 4
W = 256
COLS = NDET * W
CAPS = (16,)
MESH = pl.DeviceIdType.MESH
F32 = jnp.float32
BF16 = jnp.bfloat16


def halves(x):
    high = x.astype(BF16)
    return high, (x - high.astype(F32)).astype(BF16)


def tables(destinations, cap):
    target = destinations[:, 0]
    ids = jnp.arange(NBLK, dtype=jnp.int32)
    earlier = ids[None, :] < ids[:, None]

    def rank(key):
        return jnp.sum(((key[:, None] == key[None, :]) & earlier).astype(jnp.int32), axis=1)

    def listed(key, place, groups, size):
        match = (key[None, None, :] == jnp.arange(groups, dtype=jnp.int32)[:, None, None]) & (
            place[None, None, :] == jnp.arange(size, dtype=jnp.int32)[None, :, None]
        )
        return match.astype(jnp.int32)

    zt, yt = target // SIDE, target % SIDE
    zr, yr = rank(zt), rank(yt)
    slot = listed(target, rank(target), NDET, MOST)

    def pick(match, values):
        return jnp.sum(match * values[None, None, :], axis=2).reshape(-1)

    chosen = pick(slot, ids)
    filled = jnp.sum(slot, axis=2).reshape(-1)
    return (
        chosen,
        pick(slot, zr),
        pick(slot, yr),
        pick(listed(zt, zr, SIDE, cap), ids),
        pick(listed(yt, yr, SIDE, cap), ids),
        filled,
    )


def move_kernel(cap, chosen, zpos, ypos, zlist, ylist, raw_hbm, dark, flat, slabs, gains, *scr):
    (raw, vals, det, gmap, sa, sb, ra1, ra2, ra3, rb1, rb2, rb3, ta, tb, halo_out, halo_in, edge, part,
     got, final, gslot, raw_sem, s1, r1, s2, r2, loc, hs, hr, xs, xr, ys, yr, gs, gr) = scr
    ra, rb = (None, ra1, ra2, ra3), (None, rb1, rb2, rb3)
    me = lax.axis_index("det")
    ang = lax.axis_index("ang")
    z, y = me // SIDE, me % SIDE

    def at(dz, dy):
        return lax.rem(z + dz, SIDE) * SIDE + lax.rem(y + dy, SIDE)

    def to_det(src, dst, send, recv, where):
        return pltpu.make_async_remote_copy(src, dst, send, recv, device_id={"det": where}, device_id_type=MESH)

    def to_ang(src, dst, send, recv, where):
        return pltpu.make_async_remote_copy(src, dst, send, recv, device_id={"ang": where}, device_id_type=MESH)

    loads = [pltpu.make_async_copy(raw_hbm.at[pl.ds(16 * h, 16)], raw.at[h], raw_sem.at[h]) for h in range(2)]
    for cp in loads:
        cp.start()
    bar = pltpu.get_barrier_semaphore()
    for p in range(1, NDET):
        pl.semaphore_signal(bar, inc=1, device_id={"det": lax.rem(me + p, NDET)}, device_id_type=MESH)
    for p in range(1, 8):
        pl.semaphore_signal(bar, inc=1, device_id={"ang": lax.rem(ang + p, 8)}, device_id_type=MESH)

    low = lax.broadcasted_iota(jnp.int32, (8, W), 0) < RB
    lane = lax.broadcasted_iota(jnp.int32, (8, 128), 1)

    def project(h):
        @pl.loop(0, 16)
        def _(q):
            rows = pl.ds(pl.multiple_of(8 * q, 8), 8)
            d = dark[rows, :]
            x = -jnp.log((raw[h, :, rows, :] - d) / (flat[rows, :] - d))
            x = x.reshape(8, 2, 8, W)
            for p in range(8):
                x0, x1 = x[p, 0], x[p, 1]
                vals[2 * q, h, p] = jnp.where(low, x0, pltpu.roll(x1, RB, 0))
                vals[2 * q + 1, h, p] = jnp.where(low, pltpu.roll(x0, RB, 0), x1)

    def pack(h):
        @pl.loop(0, 8)
        def _(g):
            right = jnp.zeros((8, 128), F32)
            left = jnp.zeros((8, 128), F32)
            for i in range(32):
                x = vals[4 * g + i // 8, h, i % 8]
                here = (lane >= 4 * i) & (lane < 4 * i + 4)
                right = jnp.where(here, pltpu.roll(x[:, 128:], (4 * i + 4) % 128, 1), right)
                left = jnp.where(here, pltpu.roll(x[:, :128], 4 * i, 1), left)
            halo_out[h, 0, g] = right
            halo_out[h, 1, g] = left

    halos = []
    first = []
    second = []
    stay = []

    def halo(h):
        for side, where in ((0, lax.rem(me + 1, NDET)), (1, lax.rem(me + NDET - 1, NDET))):
            cp = to_det(halo_out.at[h, side], halo_in.at[h, side], hs.at[h, side], hr.at[h, side], where)
            cp.start()
            halos.append(cp)

    def first_hop(h):
        listing, out, into = (zlist, sa, ra) if h == 0 else (ylist, sb, rb)
        for d in (1, 3, 2):
            group = lax.rem((z if h == 0 else y) + d, SIDE)

            @pl.loop(0, cap)
            def _(c):
                out[d - 1, c] = vals[listing[group * cap + c], h]

            where = at(d, 0) if h == 0 else at(0, d)
            cp = to_det(out.at[d - 1], into[d], s1.at[h, d], r1.at[h, d], where)
            cp.start()
            first.append((h, d, cp))

    def second_hop(h, d):
        out = ta if h == 0 else tb
        col = at(SIDE - d, 0) if h == 0 else at(0, SIDE - d)
        for e in (1, 3, 2, 0):
            owner = at(0, e) if h == 0 else at(e, 0)
            for j in range(MOST):
                if d == 0:
                    out[d, e, j] = vals[chosen[owner * MOST + j], h]
                elif h == 0:
                    out[d, e, j] = ra[d][zpos[owner * MOST + j]]
                else:
                    out[d, e, j] = rb[d][ypos[owner * MOST + j]]
            if e == 0:
                cp = pltpu.make_async_copy(out.at[d, e], slabs.at[col, h], loc.at[h, d])
                stay.append(cp)
            else:
                cp = to_det(out.at[d, e], slabs.at[col, h], s2.at[h, d, e], r2.at[h, d, e], owner)
                second.append(cp)
            cp.start()

    def arrived(h, dist):
        for hh, d, cp in first:
            if hh == h and d == dist:
                cp.wait_recv()

    loads[0].wait()
    project(0)
    pack(0)
    pl.semaphore_wait(bar, NDET - 1 + 7)
    halo(0)
    first_hop(0)
    loads[1].wait()
    project(1)
    pack(1)
    halo(1)
    first_hop(1)
    second_hop(0, 0)
    second_hop(1, 0)

    src = lax.broadcasted_iota(jnp.int32, (W, W), 0)
    dst = lax.broadcasted_iota(jnp.int32, (W, W), 1)
    band = (jnp.abs(src - dst) <= SMW).astype(BF16)
    erow = lax.broadcasted_iota(jnp.int32, (128, W), 0)
    ecol = lax.broadcasted_iota(jnp.int32, (128, W), 1)
    at_left = (erow < 4) & (ecol <= erow)
    at_right = (erow >= 4) & (erow < 8) & (W + (erow - 4) - ecol <= SMW)
    eband = (at_left | at_right).astype(BF16)
    col = me * W + lax.broadcasted_iota(jnp.int32, (8, W), 1)
    number = jnp.minimum(col + SMW, COLS - 1) - jnp.maximum(col - SMW, 0) + 1
    share = (1.0 / number.astype(F32))[None]
    for cp in halos:
        cp.wait_recv()
    for h in range(2):
        @pl.loop(0, 8)
        def _(g):
            before = jnp.where(me == 0, 0.0, halo_in[h, 0, g])
            after = jnp.where(me == NDET - 1, 0.0, halo_in[h, 1, g])
            for i in range(32):
                a = pltpu.roll(before, (128 - 4 * i) % 128, 1)
                b = pltpu.roll(after, (132 - 4 * i) % 128, 1)
                edge[i] = jnp.where(lane < 4, a, jnp.where(lane < 8, b, 0.0))
            x = jnp.concatenate([vals[4 * g + i, h] for i in range(4)], axis=0)
            xh, xl = halves(x.reshape(256, W))
            eh, el = halves(edge[...].reshape(256, 128))
            summed = (
                jnp.dot(xh, band, preferred_element_type=F32)
                + jnp.dot(xl, band, preferred_element_type=F32)
                + jnp.dot(eh, eband, preferred_element_type=F32)
                + jnp.dot(el, eband, preferred_element_type=F32)
            )
            detail = x - summed.reshape(32, 8, W) * share
            for i in range(4):
                det[4 * g + i, h] = detail[8 * i : 8 * i + 8]

    def both(s):
        return s + pltpu.roll(s, RB, 0)

    def reduce_all(step):
        sends = []
        for p in range(1, 8):
            peer = lax.rem(ang + p, 8)
            cp = to_ang(part.at[step, peer], got.at[step, p], xs.at[step, p], xr.at[step, p], peer)
            cp.start()
            sends.append(cp)
        for cp in sends:
            cp.wait_recv()
        for t in range(2):
            num = part[step, ang, 0, t]
            den = part[step, ang, 1, t]
            for p in range(1, 8):
                num = num + got[step, p, 0, t]
                den = den + got[step, p, 1, t]
            final[step, ang, t] = num / den
        gathers = []
        for p in range(1, 8):
            peer = lax.rem(ang + p, 8)
            cp = to_ang(final.at[step, ang], final.at[step, ang], ys.at[step, p], yr.at[step, p], peer)
            cp.start()
            gathers.append(cp)
        for p in range(1, 8):
            gathers[p - 1].wait_recv()

        @pl.loop(0, 8)
        def _(m):
            for t in range(2):
                tile = final[step, m, t]
                turned = pltpu.roll(tile, RB, 0)
                gmap[4 * m + 2 * t] = jnp.where(low, tile, turned)
                gmap[4 * m + 2 * t + 1] = jnp.where(low, turned, tile)

        return sends + gathers

    pending = []

    @pl.loop(0, 8)
    def _(m):
        for t in range(2):
            sums = []
            for b in range(2):
                block = 4 * m + 2 * t + b
                sums.append(both(jnp.sum(det[block, 0], axis=0) + jnp.sum(det[block, 1], axis=0)))
            part[0, m, 0, t] = jnp.where(low, sums[0], sums[1])
            part[0, m, 1, t] = jnp.full((8, W), 32.0, F32)

    pending += reduce_all(0)
    for step in range(1, ITERS + 1):
        @pl.loop(0, 8)
        def _(m):
            for t in range(2):
                nums, dens = [], []
                for b in range(2):
                    block = 4 * m + 2 * t + b
                    gain = gmap[block][None]
                    num = jnp.zeros((8, W), F32)
                    den = jnp.zeros((8, W), F32)
                    for h in range(2):
                        d = det[block, h]
                        scaled = (d - gain) / 0.2
                        weight = 1.0 / (1.0 + scaled * scaled)
                        num = num + jnp.sum(weight * d, axis=0)
                        den = den + jnp.sum(weight, axis=0)
                    nums.append(both(num))
                    dens.append(both(den))
                part[step, m, 0, t] = jnp.where(low, nums[0], nums[1])
                part[step, m, 1, t] = jnp.where(low, dens[0], dens[1])

        pending += reduce_all(step)
        if step < ITERS:
            for d in (1, 3, 2)[0 : 2] if step == 1 else (2,):
                for h in range(2):
                    arrived(h, d)
                    second_hop(h, d)

    give = []
    for p in range(NDET):
        owner = lax.rem(me + p, NDET)
        for t in range(2):
            a = gmap[chosen[owner * MOST + 2 * t]]
            b = gmap[chosen[owner * MOST + 2 * t + 1]]
            gslot[p, t] = jnp.where(low, a, b)
        if p == 0:
            cp = pltpu.make_async_copy(gslot.at[p], gains.at[me], gs.at[p])
            stay.append(cp)
        else:
            cp = to_det(gslot.at[p], gains.at[me], gs.at[p], gr.at[p], owner)
            give.append(cp)
        cp.start()

    for cp in give + second:
        cp.wait_recv()
    for cp in stay:
        cp.wait()
    for cp in give + second + halos + pending + [c for _, _, c in first]:
        cp.wait_send()


def move(cap, chosen, zpos, ypos, zlist, ylist, raw, dark, flat):
    chunk = (8, 8, W)
    dma = pltpu.SemaphoreType.DMA
    scratch = [
        pltpu.VMEM((2, 16, 128, W), F32),
        pltpu.VMEM((NBLK, 2) + chunk, F32),
        pltpu.VMEM((NBLK, 2) + chunk, F32),
        pltpu.VMEM((NBLK, 8, W), F32),
        pltpu.VMEM((3, cap) + chunk, F32),
        pltpu.VMEM((3, cap) + chunk, F32),
    ]
    scratch += [pltpu.VMEM((cap,) + chunk, F32) for _ in range(6)]
    scratch += [
        pltpu.VMEM((4, 4, MOST) + chunk, F32),
        pltpu.VMEM((4, 4, MOST) + chunk, F32),
        pltpu.VMEM((2, 2, 8, 8, 128), F32),
        pltpu.VMEM((2, 2, 8, 8, 128), F32),
        pltpu.VMEM((32, 8, 128), F32),
        pltpu.VMEM((ITERS + 1, 8, 2, 2, 8, W), F32),
        pltpu.VMEM((ITERS + 1, 8, 2, 2, 8, W), F32),
        pltpu.VMEM((ITERS + 1, 8, 2, 8, W), F32),
        pltpu.VMEM((NDET, 2, 8, W), F32),
        dma((2,)),
        dma((2, 4)), dma((2, 4)),
        dma((2, 4, 4)), dma((2, 4, 4)),
        dma((2, 4)),
        dma((2, 2)), dma((2, 2)),
        dma((ITERS + 1, 8)), dma((ITERS + 1, 8)), dma((ITERS + 1, 8)), dma((ITERS + 1, 8)),
        dma((NDET,)), dma((NDET,)),
    ]
    smem = pl.BlockSpec(memory_space=pltpu.SMEM)
    vmem = pl.BlockSpec(memory_space=pltpu.VMEM)
    hbm = pl.BlockSpec(memory_space=pl.ANY)
    return pl.pallas_call(
        functools.partial(move_kernel, cap),
        out_shape=(
            jax.ShapeDtypeStruct((NDET, 2, MOST) + chunk, F32),
            jax.ShapeDtypeStruct((NDET, 2, 8, W), F32),
        ),
        in_specs=[smem] * 5 + [hbm, vmem, vmem],
        out_specs=(hbm, hbm),
        scratch_shapes=scratch,
        compiler_params=pltpu.CompilerParams(
            collective_id=cap, has_side_effects=True, vmem_limit_bytes=56 * 2**20
        ),
        name=f"move{cap}",
    )(chosen, zpos, ypos, zlist, ylist, raw, dark, flat)


def rebin_kernel(filled, slabs_hbm, gains, offsets, weights, out, slabs, xh, xl, eh, el, sems):
    c = pl.program_id(0)
    me = lax.axis_index("det")

    def load(i):
        return pltpu.make_async_copy(slabs_hbm.at[i], slabs.at[i], sems.at[i])

    @pl.when(c == 0)
    def _():
        @pl.loop(0, NDET)
        def _(i):
            load(i).start()

        load(0).wait()

    @pl.when(c < NDET - 1)
    def _():
        load(c + 1).wait()

    rel = offsets[...] - c * W
    wts = weights[...]
    row = lax.broadcasted_iota(jnp.int32, (W, W), 0)

    def coefficients(place):
        total = jnp.zeros((W, W), F32)
        for k in range(BW):
            total = jnp.where(place == rel + k, wts[k : k + 1], total)
        return halves(total)

    mh, ml = coefficients(row)
    lh, ll = coefficients(jnp.where(row < 128, row - 128, row + 128))
    low = lax.broadcasted_iota(jnp.int32, (8, W), 0) < RB
    before = jnp.maximum(c - 1, 0)
    after = jnp.minimum(c + 1, NDET - 1)

    def gain(chunk, j):
        tile = gains[chunk, j // 2]
        turned = pltpu.roll(tile, RB, 0)
        return jnp.where(low, tile, turned) if j % 2 == 0 else jnp.where(low, turned, tile)

    for j in range(MOST):
        on = filled[me * MOST + j].astype(F32)
        g = gain(c, j) * on
        gl = gain(before, j)[:, 128:] * on
        gr = gain(after, j)[:, :128] * on
        for h in range(2):
            rows = pl.ds((h * MOST + j) * 64, 64)
            x = slabs[c, h, j] * on - g[None]
            a, b = halves(x.reshape(64, W))
            xh[rows, :] = a
            xl[rows, :] = b
            a, b = halves((slabs[before, h, j, :, :, 128:] * on - gl[None]).reshape(64, 128))
            eh[rows, :128] = a
            el[rows, :128] = b
            a, b = halves((slabs[after, h, j, :, :, :128] * on - gr[None]).reshape(64, 128))
            eh[rows, 128:] = a
            el[rows, 128:] = b
    acc = (
        jnp.dot(xh[...], mh, preferred_element_type=F32)
        + jnp.dot(xl[...], mh, preferred_element_type=F32)
        + jnp.dot(xh[...], ml, preferred_element_type=F32)
        + jnp.dot(eh[...], lh, preferred_element_type=F32)
        + jnp.dot(el[...], lh, preferred_element_type=F32)
        + jnp.dot(eh[...], ll, preferred_element_type=F32)
    )
    for h in range(2):
        for j in range(MOST):
            i = (h * MOST + j) * 64
            out[16 * h : 16 * h + 16, j] = acc[i : i + 64].reshape(16, RB, W)


def rebin(filled, slabs, gains, offsets, weights):
    return pl.pallas_call(
        rebin_kernel,
        grid=(NDET,),
        out_shape=jax.ShapeDtypeStruct((32, MOST, RB, COLS), F32),
        in_specs=[
            pl.BlockSpec(memory_space=pltpu.SMEM),
            pl.BlockSpec(memory_space=pl.ANY),
            pl.BlockSpec((NDET, 2, 8, W), lambda c: (0, 0, 0, 0)),
            pl.BlockSpec((1, W), lambda c: (0, c)),
            pl.BlockSpec((BW, W), lambda c: (0, c)),
        ],
        out_specs=pl.BlockSpec((32, MOST, RB, W), lambda c: (0, 0, 0, c)),
        scratch_shapes=[
            pltpu.VMEM((NDET, 2, MOST, 8, 8, W), F32),
            pltpu.VMEM((512, W), BF16),
            pltpu.VMEM((512, W), BF16),
            pltpu.VMEM((512, W), BF16),
            pltpu.VMEM((512, W), BF16),
            pltpu.SemaphoreType.DMA((NDET,)),
        ],
        compiler_params=pltpu.CompilerParams(vmem_limit_bytes=56 * 2**20),
        name="rebin",
    )(filled, slabs, gains, offsets.reshape(1, COLS), weights)


def body(raw_counts, dark_field, flat_field, destinations, band_offsets, band_weights):
    target = destinations[:, 0]
    if len(CAPS) == 1:
        *listing, filled = tables(destinations, CAPS[0])
        slabs, gains = move(CAPS[0], *listing, raw_counts, dark_field, flat_field)
    else:
        sides = jnp.concatenate([target // SIDE, SIDE + target % SIDE])
        load = jnp.max(jnp.sum((sides[:, None] == jnp.arange(2 * SIDE)[None, :]).astype(jnp.int32), axis=0))
        branch = sum((load > cap).astype(jnp.int32) for cap in CAPS[:-1])
        filled = tables(destinations, CAPS[-1])[-1]

        def with_cap(cap):
            return lambda dest, *arrays: move(cap, *tables(dest, cap)[:-1], *arrays)

        slabs, gains = lax.switch(
            branch, [with_cap(cap) for cap in CAPS], destinations, raw_counts, dark_field, flat_field
        )
    return rebin(filled, slabs, gains, band_offsets, band_weights)


def solution(mesh):
    placed = (P("ang", None, "det"), P(None, "det"), P(None, "det"), P(), P(), P())
    return jax.shard_map(
        body, mesh=mesh, in_specs=placed, out_specs=P("ang", "det", None, None), check_vma=False
    )
```

time: 527 us -> 135 us (0.26); the launches traced: 521 us -> 135 us
  waiting for transfers between devices: 366 us -> 0 us
  Pallas kernels: 0 us -> 127 us
  other arithmetic: 91.8 us -> 3.79 us
  local copies, waits for them, and re-layouts: 37.1 us -> 3.95 us
  between operations: 13.3 us -> 0.03 us
  starting transfers between devices: 12.4 us -> 0 us
    psum x4 -> x0, waiting for transfers between devices: 242 us -> none  [the longest x3 178 us: body(): total_all, weighted_all = lax.psum((weight_total, weighted), 'ang')]
    pallas_call x0 -> x2, Pallas kernels: none -> 127 us  [the longest x1 110 us: move(): pl.pallas_call(functools.partial(move_kernel, cap), out_shape=(jax.ShapeD...]
    all_to_all x1 -> x0, waiting for transfers between devices: 120 us -> none  [body(): lax.all_to_all(picked, 'det', split_axis=1, concat_axis=4, tiled=True)]
    reshape x1 -> x0, other arithmetic: 36.4 us -> none  [body(): return moved.reshape(ang_dev, MOST, RB, total_cols)]
    reduce_sum x6 -> x5, other arithmetic: 34.1 us -> 1.76 us  [the longest x2 1.09 us: rank(): jnp.sum(((key[:, None] == key[None, :]) & earlier).astype(jnp.int32), axi...]
    mul x1 -> x0, other arithmetic: 8.87 us -> none  [slot_blocks(): return picked * filled[None, :, :, None, None].astype(jnp.float32)]
    reshape x2 -> x6, local copies, waits for them, and re-layouts: 12.3 us -> 3.62 us  [the longest x5 3 us: pick(): return jnp.sum(match * values[None, None, :], axis=2).reshape(-1)]
    unnamed x14 -> x0, local copies, waits for them, and re-layouts: 7.55 us -> none
  transfers between devices with their start and end apart: 7 -> 0, of which waited for: 7 -> 0; matrix products, arithmetic and copies ran while one was open for 0% -> 0% of each run, Pallas kernels for 0% -> 0%
where the time goes in v1:
time: 135 us
  Pallas kernels  127 us (94%)
  local copies, waits for them, and re-layouts  3.95 us (3%)
  other arithmetic  3.79 us (3%)
    pallas_call x1, Pallas kernels, move(): pl.pallas_call(functools.partial(move_kernel, cap), out_shape=(jax.ShapeD...  110 us
    pallas_call x1, Pallas kernels, rebin(): pl.pallas_call(rebin_kernel, grid=(NDET,), out_shape=jax.ShapeDtypeStruct...  17.2 us
    reshape x5, local copies, waits for them, and re-layouts, pick(): return jnp.sum(match * values[None, None, :], axis=2).reshape(-1)  3 us

profile of v1, /device:TPU:0, one launch (start us, length us, event | category | flops | bytes accessed | tf_op | source)
XLA Modules:
  0.0 134.6 jit_solution(6459270107203299035)
XLA Ops:
  0.0 0.9 convert_reduce_fusion.2
  0.9 0.7 and_select_fusion.5
  1.6 0.7 fusion.8
  2.3 0.2 convert_reduce_fusion
  2.5 0.2 select_reduce_fusion
  2.6 0.6 reshape.264.ylist
  3.2 0.2 select_reduce_fusion.1
  3.4 0.6 reshape.263.zlist
  4.0 0.7 iota_compare_fusion.3
  4.6 0.4 fusion.3
  5.0 0.1 copy.10
  5.1 0.6 reshape.262.ypos
  5.7 0.1 copy.9
  5.8 0.6 reshape.261.zpos
  6.4 0.1 copy.8
  6.5 0.6 reshape.260.chosen
  7.1 0.1 copy.7
  7.1 0.6 reshape.259.filled
  7.8 109.6 %move16.1 = (f32[16,2,4,8,8,256]{5,4,3,2,1,0:T(8,128)}, f32[16,2,8,256]{3,2,1,0:T(8,128)}) custom-call(s32[64]{0:T(128)} %reshape.260.chosen, s32[64]{0:T(128)} %reshape.261.zpos, s32[64]{0:T(128)} %reshape.262.ypos, s32[64]{0:T(128)} %reshape.263.zlist, s32[64]{0:T(128)} %reshape.264.ylist, f32[32,128,256]{2,1,0:T(8,128)} %raw_hbm.1, f32[128,256]{1,0:T(8,128)} %dark.1, ...), custom_call_target="tpu_custom_call" | custom-call | tf_op jit(solution)/shard_map/move16/pallas_call | solution.py:352
  117.4 17.2 %rebin.1 = f32[32,4,4,4096]{3,2,1,0:T(4,128)} custom-call(s32[64]{0:T(128)} %reshape.259.filled, f32[16,2,4,8,8,256]{5,4,3,2,1,0:T(8,128)} %get-tuple-element.7.slabs_hbm, f32[16,2,8,256]{3,2,1,0:T(8,128)} %get-tuple-element.8.gains, s32[1,4096]{1,0:T(1,128)} %bitcast.12, f32[4,4096]{1,0:T(4,128)} %weights.1), custom_call_target="tpu_custom_call" | custom-call | tf_op jit(solution)/shard_map/rebin/pallas_call | solution.py:440
  (4 shorter events, 0.0 us)

commit v2 on v1

--- a/solution.py
+++ b/solution.py
@@ -17,7 +17,7 @@
 SIDE = 4
 W = 256
 COLS = NDET * W
-CAPS = (16,)
+CAPS = (9, 10, 11, 16)
 MESH = pl.DeviceIdType.MESH
 F32 = jnp.float32
 BF16 = jnp.bfloat16
@@ -28,40 +28,55 @@
     return high, (x - high.astype(F32)).astype(BF16)
 
 
-def tables(destinations, cap):
-    target = destinations[:, 0]
-    ids = jnp.arange(NBLK, dtype=jnp.int32)
-    earlier = ids[None, :] < ids[:, None]
-
-    def rank(key):
-        return jnp.sum(((key[:, None] == key[None, :]) & earlier).astype(jnp.int32), axis=1)
-
-    def listed(key, place, groups, size):
-        match = (key[None, None, :] == jnp.arange(groups, dtype=jnp.int32)[:, None, None]) & (
-            place[None, None, :] == jnp.arange(size, dtype=jnp.int32)[None, :, None]
-        )
-        return match.astype(jnp.int32)
-
-    zt, yt = target // SIDE, target % SIDE
-    zr, yr = rank(zt), rank(yt)
-    slot = listed(target, rank(target), NDET, MOST)
-
-    def pick(match, values):
-        return jnp.sum(match * values[None, None, :], axis=2).reshape(-1)
-
-    chosen = pick(slot, ids)
-    filled = jnp.sum(slot, axis=2).reshape(-1)
-    return (
-        chosen,
-        pick(slot, zr),
-        pick(slot, yr),
-        pick(listed(zt, zr, SIDE, cap), ids),
-        pick(listed(yt, yr, SIDE, cap), ids),
-        filled,
-    )
-
-
-def move_kernel(cap, chosen, zpos, ypos, zlist, ylist, raw_hbm, dark, flat, slabs, gains, *scr):
+CHOSEN, ZPOS, YPOS, FILLED, ZLIST, YLIST, PLAN = 0, 64, 128, 192, 256, 320, 384
+LIST = 16
+
+
+def plan_kernel(target, plan, branch, count):
+    @pl.loop(0, PLAN // 16)
+    def _(i):
+        for k in range(16):
+            plan[16 * i + k] = 0
+
+    for k in range(NDET + 2 * SIDE):
+        count[k] = 0
+
+    @pl.loop(0, NBLK)
+    def _(b):
+        owner = target[b]
+        zg = NDET + owner // SIDE
+        yg = NDET + SIDE + owner % SIDE
+        place, zp, yp = count[owner], count[zg], count[yg]
+        count[owner] = place + 1
+        count[zg] = zp + 1
+        count[yg] = yp + 1
+        slot = owner * MOST + place
+        plan[CHOSEN + slot] = b
+        plan[ZPOS + slot] = zp
+        plan[YPOS + slot] = yp
+        plan[FILLED + slot] = 1
+        plan[ZLIST + (zg - NDET) * LIST + zp] = b
+        plan[YLIST + (yg - NDET - SIDE) * LIST + yp] = b
+
+    most = count[NDET]
+    for k in range(1, 2 * SIDE):
+        most = jnp.maximum(most, count[NDET + k])
+    branch[0] = sum((most > cap).astype(jnp.int32) for cap in CAPS[:-1]) + jnp.int32(0)
+
+
+def make_plan(destinations):
+    smem = pl.BlockSpec(memory_space=pltpu.SMEM)
+    return pl.pallas_call(
+        plan_kernel,
+        out_shape=(jax.ShapeDtypeStruct((PLAN,), jnp.int32), jax.ShapeDtypeStruct((1,), jnp.int32)),
+        in_specs=[smem],
+        out_specs=(smem, smem),
+        scratch_shapes=[pltpu.SMEM((NDET + 2 * SIDE,), jnp.int32)],
+        name="plan",
+    )(destinations.reshape(NBLK))
+
+
+def move_kernel(cap, plan, raw_hbm, dark, flat, slabs, gains, *scr):
     (raw, vals, det, gmap, sa, sb, ra1, ra2, ra3, rb1, rb2, rb3, ta, tb, halo_out, halo_in, edge, part,
      got, final, gslot, raw_sem, s1, r1, s2, r2, loc, hs, hr, xs, xr, ys, yr, gs, gr) = scr
     ra, rb = (None, ra1, ra2, ra3), (None, rb1, rb2, rb3)
@@ -127,13 +142,13 @@
             halos.append(cp)
 
     def first_hop(h):
-        listing, out, into = (zlist, sa, ra) if h == 0 else (ylist, sb, rb)
+        listing, out, into = (ZLIST, sa, ra) if h == 0 else (YLIST, sb, rb)
         for d in (1, 3, 2):
             group = lax.rem((z if h == 0 else y) + d, SIDE)
 
             @pl.loop(0, cap)
             def _(c):
-                out[d - 1, c] = vals[listing[group * cap + c], h]
+                out[d - 1, c] = vals[plan[listing + group * LIST + c], h]
 
             where = at(d, 0) if h == 0 else at(0, d)
             cp = to_det(out.at[d - 1], into[d], s1.at[h, d], r1.at[h, d], where)
@@ -147,11 +162,11 @@
             owner = at(0, e) if h == 0 else at(e, 0)
             for j in range(MOST):
                 if d == 0:
-                    out[d, e, j] = vals[chosen[owner * MOST + j], h]
+                    out[d, e, j] = vals[plan[CHOSEN + owner * MOST + j], h]
                 elif h == 0:
-                    out[d, e, j] = ra[d][zpos[owner * MOST + j]]
+                    out[d, e, j] = ra[d][plan[ZPOS + owner * MOST + j]]
                 else:
-                    out[d, e, j] = rb[d][ypos[owner * MOST + j]]
+                    out[d, e, j] = rb[d][plan[YPOS + owner * MOST + j]]
             if e == 0:
                 cp = pltpu.make_async_copy(out.at[d, e], slabs.at[col, h], loc.at[h, d])
                 stay.append(cp)
@@ -297,8 +312,8 @@
     for p in range(NDET):
         owner = lax.rem(me + p, NDET)
         for t in range(2):
-            a = gmap[chosen[owner * MOST + 2 * t]]
-            b = gmap[chosen[owner * MOST + 2 * t + 1]]
+            a = gmap[plan[CHOSEN + owner * MOST + 2 * t]]
+            b = gmap[plan[CHOSEN + owner * MOST + 2 * t + 1]]
             gslot[p, t] = jnp.where(low, a, b)
         if p == 0:
             cp = pltpu.make_async_copy(gslot.at[p], gains.at[me], gs.at[p])
@@ -316,7 +331,7 @@
         cp.wait_send()
 
 
-def move(cap, chosen, zpos, ypos, zlist, ylist, raw, dark, flat):
+def move(cap, plan, raw, dark, flat):
     chunk = (8, 8, W)
     dma = pltpu.SemaphoreType.DMA
     scratch = [
@@ -355,17 +370,17 @@
             jax.ShapeDtypeStruct((NDET, 2, MOST) + chunk, F32),
             jax.ShapeDtypeStruct((NDET, 2, 8, W), F32),
         ),
-        in_specs=[smem] * 5 + [hbm, vmem, vmem],
+        in_specs=[smem, hbm, vmem, vmem],
         out_specs=(hbm, hbm),
         scratch_shapes=scratch,
         compiler_params=pltpu.CompilerParams(
             collective_id=cap, has_side_effects=True, vmem_limit_bytes=56 * 2**20
         ),
         name=f"move{cap}",
-    )(chosen, zpos, ypos, zlist, ylist, raw, dark, flat)
-
-
-def rebin_kernel(filled, slabs_hbm, gains, offsets, weights, out, slabs, xh, xl, eh, el, sems):
+    )(plan, raw, dark, flat)
+
+
+def rebin_kernel(plan, slabs_hbm, gains, offsets, weights, out, slabs, lhs, rhs, low_rhs, sems):
     c = pl.program_id(0)
     me = lax.axis_index("det")
 
@@ -378,6 +393,8 @@
         def _(i):
             load(i).start()
 
+        rhs[...] = jnp.zeros(rhs.shape, BF16)
+        low_rhs[...] = jnp.zeros(low_rhs.shape, BF16)
         load(0).wait()
 
     @pl.when(c < NDET - 1)
@@ -386,17 +403,27 @@
 
     rel = offsets[...] - c * W
     wts = weights[...]
-    row = lax.broadcasted_iota(jnp.int32, (W, W), 0)
-
-    def coefficients(place):
-        total = jnp.zeros((W, W), F32)
+
+    def coefficients(row, cols):
+        ahead = row - rel[:, cols]
+        total = jnp.zeros(ahead.shape, F32)
         for k in range(BW):
-            total = jnp.where(place == rel + k, wts[k : k + 1], total)
+            total = jnp.where(ahead == k, wts[k : k + 1, cols], total)
         return halves(total)
 
-    mh, ml = coefficients(row)
-    lh, ll = coefficients(jnp.where(row < 128, row - 128, row + 128))
+    for start, cols in ((0, slice(0, 128)), (112, slice(128, 256))):
+        high, small = coefficients(start + lax.broadcasted_iota(jnp.int32, (144, 128), 0), cols)
+        rhs[start : start + 144, cols] = high
+        rhs[W + start : W + start + 144, cols] = high
+        low_rhs[start : start + 144, cols] = small
+    row = lax.broadcasted_iota(jnp.int32, (16, W), 0)
+    high, small = coefficients(jnp.where(row < 8, row - 8, row + (W - 8)), slice(0, W))
+    rhs[2 * W : 2 * W + 16, :] = high
+    rhs[2 * W + 16 : 2 * W + 32, :] = high
+    rhs[2 * W + 32 : 2 * W + 48, :] = small
+
     low = lax.broadcasted_iota(jnp.int32, (8, W), 0) < RB
+    lane = lax.broadcasted_iota(jnp.int32, (1, 1, 128), 2)
     before = jnp.maximum(c - 1, 0)
     after = jnp.minimum(c + 1, NDET - 1)
 
@@ -406,37 +433,31 @@
         return jnp.where(low, tile, turned) if j % 2 == 0 else jnp.where(low, turned, tile)
 
     for j in range(MOST):
-        on = filled[me * MOST + j].astype(F32)
-        g = gain(c, j) * on
-        gl = gain(before, j)[:, 128:] * on
-        gr = gain(after, j)[:, :128] * on
+        on = plan[FILLED + me * MOST + j].astype(F32)
+        g = (gain(c, j) * on)[None]
+        ge = (jnp.where(lane[0] >= 64, gain(before, j)[:, 128:], gain(after, j)[:, :128]) * on)[None]
         for h in range(2):
-            rows = pl.ds((h * MOST + j) * 64, 64)
-            x = slabs[c, h, j] * on - g[None]
+            rows = slice((h * MOST + j) * 64, (h * MOST + j) * 64 + 64)
+            x = slabs[c, h, j] * on - g
             a, b = halves(x.reshape(64, W))
-            xh[rows, :] = a
-            xl[rows, :] = b
-            a, b = halves((slabs[before, h, j, :, :, 128:] * on - gl[None]).reshape(64, 128))
-            eh[rows, :128] = a
-            el[rows, :128] = b
-            a, b = halves((slabs[after, h, j, :, :, :128] * on - gr[None]).reshape(64, 128))
-            eh[rows, 128:] = a
-            el[rows, 128:] = b
-    acc = (
-        jnp.dot(xh[...], mh, preferred_element_type=F32)
-        + jnp.dot(xl[...], mh, preferred_element_type=F32)
-        + jnp.dot(xh[...], ml, preferred_element_type=F32)
-        + jnp.dot(eh[...], lh, preferred_element_type=F32)
-        + jnp.dot(el[...], lh, preferred_element_type=F32)
-        + jnp.dot(eh[...], ll, preferred_element_type=F32)
-    )
+            lhs[rows, 0:W] = a
+            lhs[rows, W : 2 * W] = b
+            e = jnp.where(lane >= 64, slabs[before, h, j, :, :, 128:], slabs[after, h, j, :, :, :128])
+            e = (e * on - ge).reshape(64, 128)
+            e = jnp.where(lane[0] < 16, pltpu.roll(e, 8, 1), 0.0)
+            e = e + pltpu.roll(e, 16, 1) + pltpu.roll(e, 32, 1)
+            a, b = halves(e)
+            middle = (lane[0] >= 16) & (lane[0] < 32)
+            lhs[rows, 2 * W :] = jnp.where(middle, b.astype(F32), a.astype(F32)).astype(BF16)
     for h in range(2):
         for j in range(MOST):
-            i = (h * MOST + j) * 64
-            out[16 * h : 16 * h + 16, j] = acc[i : i + 64].reshape(16, RB, W)
-
-
-def rebin(filled, slabs, gains, offsets, weights):
+            rows = slice((h * MOST + j) * 64, (h * MOST + j) * 64 + 64)
+            acc = jnp.dot(lhs[rows, :], rhs[...], preferred_element_type=F32)
+            acc = acc + jnp.dot(lhs[rows, 0:W], low_rhs[...], preferred_element_type=F32)
+            out[16 * h : 16 * h + 16, j] = acc.reshape(16, RB, W)
+
+
+def rebin(plan, slabs, gains, offsets, weights):
     return pl.pallas_call(
         rebin_kernel,
         grid=(NDET,),
@@ -451,35 +472,22 @@
         out_specs=pl.BlockSpec((32, MOST, RB, W), lambda c: (0, 0, 0, c)),
         scratch_shapes=[
             pltpu.VMEM((NDET, 2, MOST, 8, 8, W), F32),
-            pltpu.VMEM((512, W), BF16),
-            pltpu.VMEM((512, W), BF16),
-            pltpu.VMEM((512, W), BF16),
-            pltpu.VMEM((512, W), BF16),
+            pltpu.VMEM((512, 2 * W + 128), BF16),
+            pltpu.VMEM((2 * W + 128, W), BF16),
+            pltpu.VMEM((W, W), BF16),
             pltpu.SemaphoreType.DMA((NDET,)),
         ],
         compiler_params=pltpu.CompilerParams(vmem_limit_bytes=56 * 2**20),
         name="rebin",
-    )(filled, slabs, gains, offsets.reshape(1, COLS), weights)
+    )(plan, slabs, gains, offsets.reshape(1, COLS), weights)
 
 
 def body(raw_counts, dark_field, flat_field, destinations, band_offsets, band_weights):
-    target = destinations[:, 0]
-    if len(CAPS) == 1:
-        *listing, filled = tables(destinations, CAPS[0])
-        slabs, gains = move(CAPS[0], *listing, raw_counts, dark_field, flat_field)
-    else:
-        sides = jnp.concatenate([target // SIDE, SIDE + target % SIDE])
-        load = jnp.max(jnp.sum((sides[:, None] == jnp.arange(2 * SIDE)[None, :]).astype(jnp.int32), axis=0))
-        branch = sum((load > cap).astype(jnp.int32) for cap in CAPS[:-1])
-        filled = tables(destinations, CAPS[-1])[-1]
-
-        def with_cap(cap):
-            return lambda dest, *arrays: move(cap, *tables(dest, cap)[:-1], *arrays)
-
-        slabs, gains = lax.switch(
-            branch, [with_cap(cap) for cap in CAPS], destinations, raw_counts, dark_field, flat_field
-        )
-    return rebin(filled, slabs, gains, band_offsets, band_weights)
+    plan, branch = make_plan(destinations)
+    slabs, gains = lax.switch(
+        branch[0], [functools.partial(move, cap) for cap in CAPS], plan, raw_counts, dark_field, flat_field
+    )
+    return rebin(plan, slabs, gains, band_offsets, band_weights)
 
 
 def solution(mesh):

time: 135 us -> 114 us (0.84)
  Pallas kernels: 127 us -> 112 us
  local copies, waits for them, and re-layouts: 3.95 us -> 0 us
  other arithmetic: 3.79 us -> 0 us
    pallas_call x1, Pallas kernels: 110 us -> 92.6 us  [move(): pl.pallas_call(functools.partial(move_kernel, cap), out_shape=(jax.ShapeD...]
    reshape x6 -> x0, local copies, waits for them, and re-layouts: 3.62 us -> none  [the longest x5 3 us: pick(): return jnp.sum(match * values[None, None, :], axis=2).reshape(-1)]
    pallas_call x0 -> x1, Pallas kernels: none -> 2.4 us  [make_plan(): pl.pallas_call(plan_kernel, out_shape=(jax.ShapeDtypeStruct((PLAN,), jnp....]
    reduce_sum x5 -> x0, other arithmetic: 1.76 us -> none  [the longest x2 1.09 us: rank(): jnp.sum(((key[:, None] == key[None, :]) & earlier).astype(jnp.int32), axi...]
    eq x6 -> x0, other arithmetic: 1.36 us -> none  [the longest x2 0.67 us: listed(): key[None, None, :] == jnp.arange(groups, dtype=jnp.int32)[:, None, None]]
where the time goes in v2:
time: 114 us; the launch traced here: 113 us
  Pallas kernels  112 us (98%)
    pallas_call x1, Pallas kernels, move(): pl.pallas_call(functools.partial(move_kernel, cap), out_shape=(jax.ShapeD...  92.6 us
    pallas_call x1, Pallas kernels, rebin(): pl.pallas_call(rebin_kernel, grid=(NDET,), out_shape=jax.ShapeDtypeStruct...  17.3 us
    pallas_call x1, Pallas kernels, make_plan(): pl.pallas_call(plan_kernel, out_shape=(jax.ShapeDtypeStruct((PLAN,), jnp....  2.4 us

profile of v2, /device:TPU:0, one launch (start us, length us, event | category | flops | bytes accessed | tf_op | source)
XLA Modules:
  0.0 113.4 jit_solution(7083486430268371963)
XLA Ops:
  0.0 2.4 %plan.1 = (s32[384]{0:T(512)S(1)}, s32[1]{0:T(128)}) custom-call(s32[32]{0:T(128)} %bitcast.4), custom_call_target="tpu_custom_call" | custom-call | tf_op jit(solution)/shard_map/plan/pallas_call | solution.py:69
  3.1 92.8 %conditional.1 = ((f32[16,2,4,8,8,256]{5,4,3,2,1,0:T(8,128)}, f32[16,2,8,256]{3,2,1,0:T(8,128)S(1)})) conditional(s32[]{:T(128)} %bitcast.1, (s32[384]{0:T(512)S(1)}, f32[32,128,256]{2,1,0:T(8,128)}, f32[128,256]{1,0:T(8,128)}, f32[128,256]{1,0:T(8,128)}) %tuple.17, (s32[384]{0:T(512)S(1)}, ...), branch_computations={%region_0.0_spmd, %region_1.0_spmd, %region_2.0_spmd, %region_3.0_... | conditional | bytes 8 | solution.py:487
  3.1 92.6 %move10.1 = (f32[16,2,4,8,8,256]{5,4,3,2,1,0:T(8,128)}, f32[16,2,8,256]{3,2,1,0:T(8,128)S(1)}) custom-call(s32[384]{0:T(512)S(1)} %get-tuple-element.41.plan, f32[32,128,256]{2,1,0:T(8,128)} %get-tuple-element.42.raw_hbm, f32[128,256]{1,0:T(8,128)} %get-tuple-element.43.dark, f32[128,256]{1,0:T(8,128)} %get-tuple-element.44.flat), custom_call_target="tpu_custom_call" | custom-call | tf_op jit(solution)/shard_map/cond/branch_1_fun/move10/pallas_call | solution.py:367
  95.9 17.3 %rebin.1 = f32[32,4,4,4096]{3,2,1,0:T(4,128)} custom-call(s32[384]{0:T(512)S(1)} %get-tuple-element.57.plan, f32[16,2,4,8,8,256]{5,4,3,2,1,0:T(8,128)} %get-tuple-element.59.slabs_hbm, f32[16,2,8,256]{3,2,1,0:T(8,128)S(1)} %get-tuple-element.60.gains, s32[1,4096]{1,0:T(1,128)} %bitcast.3, f32[4,4096]{1,0:T(4,128)} %weights.1), custom_call_target="tpu_custom_call" | custom-call | tf_op jit(solution)/shard_map/rebin/pallas_call | solution.py:461

commit v3 on v2

--- a/solution.py
+++ b/solution.py
@@ -28,40 +28,34 @@
     return high, (x - high.astype(F32)).astype(BF16)
 
 
-CHOSEN, ZPOS, YPOS, FILLED, ZLIST, YLIST, PLAN = 0, 64, 128, 192, 256, 320, 384
+ZLIST, YLIST, PLAN = 64, 128, 192
 LIST = 16
+EMPTY = NBLK + (LIST << 6) + (LIST << 11)
 
 
 def plan_kernel(target, plan, branch, count):
-    @pl.loop(0, PLAN // 16)
-    def _(i):
-        for k in range(16):
-            plan[16 * i + k] = 0
+    for i in range(PLAN):
+        plan[i] = jnp.int32(EMPTY if i < ZLIST else NBLK)
 
     for k in range(NDET + 2 * SIDE):
         count[k] = 0
 
-    @pl.loop(0, NBLK)
-    def _(b):
+    for b in range(NBLK):
         owner = target[b]
-        zg = NDET + owner // SIDE
-        yg = NDET + SIDE + owner % SIDE
+        zg = NDET + (owner >> 2)
+        yg = NDET + SIDE + (owner & 3)
         place, zp, yp = count[owner], count[zg], count[yg]
         count[owner] = place + 1
         count[zg] = zp + 1
         count[yg] = yp + 1
-        slot = owner * MOST + place
-        plan[CHOSEN + slot] = b
-        plan[ZPOS + slot] = zp
-        plan[YPOS + slot] = yp
-        plan[FILLED + slot] = 1
+        plan[owner * MOST + place] = b + (zp << 6) + (yp << 11)
         plan[ZLIST + (zg - NDET) * LIST + zp] = b
         plan[YLIST + (yg - NDET - SIDE) * LIST + yp] = b
 
     most = count[NDET]
     for k in range(1, 2 * SIDE):
         most = jnp.maximum(most, count[NDET + k])
-    branch[0] = sum((most > cap).astype(jnp.int32) for cap in CAPS[:-1]) + jnp.int32(0)
+    branch[0] = sum(((most > cap).astype(jnp.int32) for cap in CAPS[:-1]), jnp.int32(0))
 
 
 def make_plan(destinations):
@@ -78,11 +72,12 @@
 
 def move_kernel(cap, plan, raw_hbm, dark, flat, slabs, gains, *scr):
     (raw, vals, det, gmap, sa, sb, ra1, ra2, ra3, rb1, rb2, rb3, ta, tb, halo_out, halo_in, edge, part,
-     got, final, gslot, raw_sem, s1, r1, s2, r2, loc, hs, hr, xs, xr, ys, yr, gs, gr) = scr
+     got, final, gslot, ghalf, raw_sem, s1, r1, s2, r2, loc, hs, hr, xs, xr, ys, yr, gs, gr, ps, pr) = scr
     ra, rb = (None, ra1, ra2, ra3), (None, rb1, rb2, rb3)
     me = lax.axis_index("det")
     ang = lax.axis_index("ang")
     z, y = me // SIDE, me % SIDE
+    core = ang % 2
 
     def at(dz, dy):
         return lax.rem(z + dz, SIDE) * SIDE + lax.rem(y + dy, SIDE)
@@ -151,7 +146,7 @@
                 out[d - 1, c] = vals[plan[listing + group * LIST + c], h]
 
             where = at(d, 0) if h == 0 else at(0, d)
-            cp = to_det(out.at[d - 1], into[d], s1.at[h, d], r1.at[h, d], where)
+            cp = to_det(out.at[d - 1], into[d].at[pl.ds(0, cap)], s1.at[h, d], r1.at[h, d], where)
             cp.start()
             first.append((h, d, cp))
 
@@ -161,12 +156,13 @@
         for e in (1, 3, 2, 0):
             owner = at(0, e) if h == 0 else at(e, 0)
             for j in range(MOST):
+                word = plan[owner * MOST + j]
                 if d == 0:
-                    out[d, e, j] = vals[plan[CHOSEN + owner * MOST + j], h]
+                    out[d, e, j] = vals[word & 63, h]
                 elif h == 0:
-                    out[d, e, j] = ra[d][plan[ZPOS + owner * MOST + j]]
+                    out[d, e, j] = ra[d][jnp.minimum((word >> 6) & 31, cap)]
                 else:
-                    out[d, e, j] = rb[d][plan[YPOS + owner * MOST + j]]
+                    out[d, e, j] = rb[d][jnp.minimum(word >> 11, cap)]
             if e == 0:
                 cp = pltpu.make_async_copy(out.at[d, e], slabs.at[col, h], loc.at[h, d])
                 stay.append(cp)
@@ -180,14 +176,20 @@
             if hh == h and d == dist:
                 cp.wait_recv()
 
+    nothing = jnp.zeros((8, 8, W), F32)
+    for h in range(2):
+        vals[NBLK, h] = nothing
+        for d in range(1, SIDE):
+            (ra, rb)[h][d][cap] = nothing
+    gmap[NBLK] = nothing[0]
     loads[0].wait()
     project(0)
     pack(0)
-    pl.semaphore_wait(bar, NDET - 1 + 7)
-    halo(0)
-    first_hop(0)
     loads[1].wait()
     project(1)
+    pl.semaphore_wait(bar, NDET - 1 + 7)
+    first_hop(0)
+    halo(0)
     pack(1)
     halo(1)
     first_hop(1)
@@ -292,7 +294,7 @@
                     den = jnp.zeros((8, W), F32)
                     for h in range(2):
                         d = det[block, h]
-                        scaled = (d - gain) / 0.2
+                        scaled = (d - gain) * 5.0
                         weight = 1.0 / (1.0 + scaled * scaled)
                         num = num + jnp.sum(weight * d, axis=0)
                         den = den + jnp.sum(weight, axis=0)
@@ -302,8 +304,8 @@
                 part[step, m, 1, t] = jnp.where(low, dens[0], dens[1])
 
         pending += reduce_all(step)
-        if step < ITERS:
-            for d in (1, 3, 2)[0 : 2] if step == 1 else (2,):
+        if step == 1:
+            for d in (1, 3):
                 for h in range(2):
                     arrived(h, d)
                     second_hop(h, d)
@@ -311,23 +313,35 @@
     give = []
     for p in range(NDET):
         owner = lax.rem(me + p, NDET)
-        for t in range(2):
-            a = gmap[plan[CHOSEN + owner * MOST + 2 * t]]
-            b = gmap[plan[CHOSEN + owner * MOST + 2 * t + 1]]
-            gslot[p, t] = jnp.where(low, a, b)
+        a = gmap[plan[owner * MOST + 2 * core] & 63]
+        b = gmap[plan[owner * MOST + 2 * core + 1] & 63]
+        gslot[p] = jnp.where(low, a, b)
         if p == 0:
-            cp = pltpu.make_async_copy(gslot.at[p], gains.at[me], gs.at[p])
-            stay.append(cp)
+            cp = pltpu.make_async_copy(gslot.at[p], ghalf.at[me], gs.at[p])
         else:
-            cp = to_det(gslot.at[p], gains.at[me], gs.at[p], gr.at[p], owner)
+            cp = to_det(gslot.at[p], ghalf.at[me], gs.at[p], gr.at[p], owner)
             give.append(cp)
         cp.start()
-
-    for cp in give + second:
+        if p == 0:
+            mine = cp
+    for h in range(2):
+        arrived(h, 2)
+        second_hop(h, 2)
+    mine.wait()
+    for cp in give:
+        cp.wait_recv()
+    swap = to_ang(ghalf, gains.at[core], ps, pr, ang + 1 - 2 * core)
+    swap.start()
+    keep = pltpu.make_async_copy(ghalf, gains.at[core], gs.at[0])
+    keep.start()
+    stay.append(keep)
+
+    swap.wait_recv()
+    for cp in second:
         cp.wait_recv()
     for cp in stay:
         cp.wait()
-    for cp in give + second + halos + pending + [c for _, _, c in first]:
+    for cp in [swap] + give + second + halos + pending + [c for _, _, c in first]:
         cp.wait_send()
 
 
@@ -336,13 +350,13 @@
     dma = pltpu.SemaphoreType.DMA
     scratch = [
         pltpu.VMEM((2, 16, 128, W), F32),
+        pltpu.VMEM((NBLK + 1, 2) + chunk, F32),
         pltpu.VMEM((NBLK, 2) + chunk, F32),
-        pltpu.VMEM((NBLK, 2) + chunk, F32),
-        pltpu.VMEM((NBLK, 8, W), F32),
+        pltpu.VMEM((NBLK + 1, 8, W), F32),
         pltpu.VMEM((3, cap) + chunk, F32),
         pltpu.VMEM((3, cap) + chunk, F32),
     ]
-    scratch += [pltpu.VMEM((cap,) + chunk, F32) for _ in range(6)]
+    scratch += [pltpu.VMEM((cap + 1,) + chunk, F32) for _ in range(6)]
     scratch += [
         pltpu.VMEM((4, 4, MOST) + chunk, F32),
         pltpu.VMEM((4, 4, MOST) + chunk, F32),
@@ -352,14 +366,15 @@
         pltpu.VMEM((ITERS + 1, 8, 2, 2, 8, W), F32),
         pltpu.VMEM((ITERS + 1, 8, 2, 2, 8, W), F32),
         pltpu.VMEM((ITERS + 1, 8, 2, 8, W), F32),
-        pltpu.VMEM((NDET, 2, 8, W), F32),
+        pltpu.VMEM((NDET, 8, W), F32),
+        pltpu.VMEM((NDET, 8, W), F32),
         dma((2,)),
         dma((2, 4)), dma((2, 4)),
         dma((2, 4, 4)), dma((2, 4, 4)),
         dma((2, 4)),
         dma((2, 2)), dma((2, 2)),
         dma((ITERS + 1, 8)), dma((ITERS + 1, 8)), dma((ITERS + 1, 8)), dma((ITERS + 1, 8)),
-        dma((NDET,)), dma((NDET,)),
+        dma((NDET,)), dma((NDET,)), dma(()), dma(()),
     ]
     smem = pl.BlockSpec(memory_space=pltpu.SMEM)
     vmem = pl.BlockSpec(memory_space=pltpu.VMEM)
@@ -368,7 +383,7 @@
         functools.partial(move_kernel, cap),
         out_shape=(
             jax.ShapeDtypeStruct((NDET, 2, MOST) + chunk, F32),
-            jax.ShapeDtypeStruct((NDET, 2, 8, W), F32),
+            jax.ShapeDtypeStruct((2, NDET, 8, W), F32),
         ),
         in_specs=[smem, hbm, vmem, vmem],
         out_specs=(hbm, hbm),
@@ -380,106 +395,118 @@
     )(plan, raw, dark, flat)
 
 
-def rebin_kernel(plan, slabs_hbm, gains, offsets, weights, out, slabs, lhs, rhs, low_rhs, sems):
-    c = pl.program_id(0)
-    me = lax.axis_index("det")
-
-    def load(i):
-        return pltpu.make_async_copy(slabs_hbm.at[i], slabs.at[i], sems.at[i])
-
-    @pl.when(c == 0)
+def rebin_kernel(slabs_hbm, gains, offsets, weights, out, slabs, lhs0, lhs1, rhs0, rhs1, low0, low1, sems):
+    i = pl.program_id(0)
+    pair = ((lhs0, rhs0, low0), (lhs1, rhs1, low1))
+
+    def load(n):
+        return pltpu.make_async_copy(slabs_hbm.at[n], slabs.at[n], sems.at[n])
+
+    low = lax.broadcasted_iota(jnp.int32, (8, W), 0) < RB
+    lane = lax.broadcasted_iota(jnp.int32, (8, 128), 1)[None]
+    second = (lane >= 64) & (lane < 80)
+    third = (lane >= 32) & (lane < 48)
+
+    def prepare(c, lhs, rhs, low_rhs):
+        here = pl.ds(pl.multiple_of(c * W, W), W)
+        rel = offsets[:, here] - c * W
+        wts = weights[:, here]
+
+        def coefficients(row, cols):
+            ahead = row - rel[:, cols]
+            total = jnp.zeros(ahead.shape, F32)
+            for k in range(BW):
+                total = jnp.where(ahead == k, wts[k : k + 1, cols], total)
+            return halves(total)
+
+        for start, cols in ((0, slice(0, 128)), (112, slice(128, 256))):
+            high, small = coefficients(start + lax.broadcasted_iota(jnp.int32, (144, 128), 0), cols)
+            rhs[start : start + 144, cols] = high
+            rhs[W + start : W + start + 144, cols] = high
+            low_rhs[start : start + 144, cols] = small
+        row = lax.broadcasted_iota(jnp.int32, (16, W), 0)
+        high, small = coefficients(jnp.where(row < 8, row - 8, row + (W - 8)), slice(0, W))
+        high32 = high.astype(F32)
+        none = jnp.zeros((8, W), F32)
+        rhs[2 * W : 2 * W + 16, :] = jnp.concatenate([high32[8:], none], axis=0).astype(BF16)
+        rhs[2 * W + 32 : 2 * W + 48, :] = small
+        rhs[2 * W + 64 : 2 * W + 80, :] = high
+        rhs[2 * W + 112 : 2 * W + 128, :] = jnp.concatenate([none, high32[:8]], axis=0).astype(BF16)
+
+        before = jnp.maximum(c - 1, 0)
+        after = jnp.minimum(c + 1, NDET - 1)
+
+        def gain(chunk, j):
+            tile = gains[j // 2, chunk]
+            turned = pltpu.roll(tile, RB, 0)
+            return jnp.where(low, tile, turned) if j % 2 == 0 else jnp.where(low, turned, tile)
+
+        for j in range(MOST):
+            g = gain(c, j)[None]
+            ge = jnp.where(lane >= 64, gain(before, j)[None, :, 128:], gain(after, j)[None, :, :128])
+            for h in range(2):
+                rows = slice((h * MOST + j) * 64, (h * MOST + j) * 64 + 64)
+                a, b = halves((slabs[c, h, j] - g).reshape(64, W))
+                lhs[rows, 0:W] = a
+                lhs[rows, W : 2 * W] = b
+                e = jnp.where(lane >= 64, slabs[before, h, j, :, :, 128:], slabs[after, h, j, :, :, :128]) - ge
+                e = jnp.where(second, pltpu.roll(e, 72, 2), jnp.where(third, pltpu.roll(e, 40, 2), e))
+                high = e.astype(BF16).astype(F32)
+                e = jnp.where(second, e - high, high)
+                lhs[rows, 2 * W :] = e.reshape(64, 128).astype(BF16)
+
+    def product(side, lhs, rhs, low_rhs):
+        acc = jnp.dot(lhs[...], rhs[...], preferred_element_type=F32)
+        acc = acc + jnp.dot(lhs[:, 0:W], low_rhs[...], preferred_element_type=F32)
+        for h in range(2):
+            for j in range(MOST):
+                rows = slice((h * MOST + j) * 64, (h * MOST + j) * 64 + 64)
+                out[16 * h : 16 * h + 16, j, :, side * W : side * W + W] = acc[rows].reshape(16, RB, W)
+
+    @pl.when(i == 0)
     def _():
         @pl.loop(0, NDET)
-        def _(i):
-            load(i).start()
-
-        rhs[...] = jnp.zeros(rhs.shape, BF16)
-        low_rhs[...] = jnp.zeros(low_rhs.shape, BF16)
+        def _(n):
+            load(n).start()
+
+        for _, rhs, low_rhs in pair:
+            rhs[...] = jnp.zeros(rhs.shape, BF16)
+            low_rhs[...] = jnp.zeros(low_rhs.shape, BF16)
         load(0).wait()
-
-    @pl.when(c < NDET - 1)
+        load(1).wait()
+        prepare(0, *pair[0])
+
+    @pl.when(i < NDET // 2 - 1)
     def _():
-        load(c + 1).wait()
-
-    rel = offsets[...] - c * W
-    wts = weights[...]
-
-    def coefficients(row, cols):
-        ahead = row - rel[:, cols]
-        total = jnp.zeros(ahead.shape, F32)
-        for k in range(BW):
-            total = jnp.where(ahead == k, wts[k : k + 1, cols], total)
-        return halves(total)
-
-    for start, cols in ((0, slice(0, 128)), (112, slice(128, 256))):
-        high, small = coefficients(start + lax.broadcasted_iota(jnp.int32, (144, 128), 0), cols)
-        rhs[start : start + 144, cols] = high
-        rhs[W + start : W + start + 144, cols] = high
-        low_rhs[start : start + 144, cols] = small
-    row = lax.broadcasted_iota(jnp.int32, (16, W), 0)
-    high, small = coefficients(jnp.where(row < 8, row - 8, row + (W - 8)), slice(0, W))
-    rhs[2 * W : 2 * W + 16, :] = high
-    rhs[2 * W + 16 : 2 * W + 32, :] = high
-    rhs[2 * W + 32 : 2 * W + 48, :] = small
-
-    low = lax.broadcasted_iota(jnp.int32, (8, W), 0) < RB
-    lane = lax.broadcasted_iota(jnp.int32, (1, 1, 128), 2)
-    before = jnp.maximum(c - 1, 0)
-    after = jnp.minimum(c + 1, NDET - 1)
-
-    def gain(chunk, j):
-        tile = gains[chunk, j // 2]
-        turned = pltpu.roll(tile, RB, 0)
-        return jnp.where(low, tile, turned) if j % 2 == 0 else jnp.where(low, turned, tile)
-
-    for j in range(MOST):
-        on = plan[FILLED + me * MOST + j].astype(F32)
-        g = (gain(c, j) * on)[None]
-        ge = (jnp.where(lane[0] >= 64, gain(before, j)[:, 128:], gain(after, j)[:, :128]) * on)[None]
-        for h in range(2):
-            rows = slice((h * MOST + j) * 64, (h * MOST + j) * 64 + 64)
-            x = slabs[c, h, j] * on - g
-            a, b = halves(x.reshape(64, W))
-            lhs[rows, 0:W] = a
-            lhs[rows, W : 2 * W] = b
-            e = jnp.where(lane >= 64, slabs[before, h, j, :, :, 128:], slabs[after, h, j, :, :, :128])
-            e = (e * on - ge).reshape(64, 128)
-            e = jnp.where(lane[0] < 16, pltpu.roll(e, 8, 1), 0.0)
-            e = e + pltpu.roll(e, 16, 1) + pltpu.roll(e, 32, 1)
-            a, b = halves(e)
-            middle = (lane[0] >= 16) & (lane[0] < 32)
-            lhs[rows, 2 * W :] = jnp.where(middle, b.astype(F32), a.astype(F32)).astype(BF16)
-    for h in range(2):
-        for j in range(MOST):
-            rows = slice((h * MOST + j) * 64, (h * MOST + j) * 64 + 64)
-            acc = jnp.dot(lhs[rows, :], rhs[...], preferred_element_type=F32)
-            acc = acc + jnp.dot(lhs[rows, 0:W], low_rhs[...], preferred_element_type=F32)
-            out[16 * h : 16 * h + 16, j] = acc.reshape(16, RB, W)
-
-
-def rebin(plan, slabs, gains, offsets, weights):
+        load(2 * i + 2).wait()
+        load(2 * i + 3).wait()
+
+    prepare(2 * i + 1, *pair[1])
+    product(0, *pair[0])
+    prepare(jnp.minimum(2 * i + 2, NDET - 1), *pair[0])
+    product(1, *pair[1])
+
+
+def rebin(slabs, gains, offsets, weights):
     return pl.pallas_call(
         rebin_kernel,
-        grid=(NDET,),
+        grid=(NDET // 2,),
         out_shape=jax.ShapeDtypeStruct((32, MOST, RB, COLS), F32),
         in_specs=[
-            pl.BlockSpec(memory_space=pltpu.SMEM),
             pl.BlockSpec(memory_space=pl.ANY),
-            pl.BlockSpec((NDET, 2, 8, W), lambda c: (0, 0, 0, 0)),
-            pl.BlockSpec((1, W), lambda c: (0, c)),
-            pl.BlockSpec((BW, W), lambda c: (0, c)),
+            pl.BlockSpec((2, NDET, 8, W), lambda c: (0, 0, 0, 0)),
+            pl.BlockSpec((1, COLS), lambda c: (0, 0)),
+            pl.BlockSpec((BW, COLS), lambda c: (0, 0)),
         ],
-        out_specs=pl.BlockSpec((32, MOST, RB, W), lambda c: (0, 0, 0, c)),
-        scratch_shapes=[
-            pltpu.VMEM((NDET, 2, MOST, 8, 8, W), F32),
-            pltpu.VMEM((512, 2 * W + 128), BF16),
-            pltpu.VMEM((2 * W + 128, W), BF16),
-            pltpu.VMEM((W, W), BF16),
-            pltpu.SemaphoreType.DMA((NDET,)),
-        ],
+        out_specs=pl.BlockSpec((32, MOST, RB, 2 * W), lambda c: (0, 0, 0, c)),
+        scratch_shapes=[pltpu.VMEM((NDET, 2, MOST, 8, 8, W), F32)]
+        + [pltpu.VMEM((512, 2 * W + 128), BF16)] * 2
+        + [pltpu.VMEM((2 * W + 128, W), BF16)] * 2
+        + [pltpu.VMEM((W, W), BF16)] * 2
+        + [pltpu.SemaphoreType.DMA((NDET,))],
         compiler_params=pltpu.CompilerParams(vmem_limit_bytes=56 * 2**20),
         name="rebin",
-    )(plan, slabs, gains, offsets.reshape(1, COLS), weights)
+    )(slabs, gains, offsets.reshape(1, COLS), weights)
 
 
 def body(raw_counts, dark_field, flat_field, destinations, band_offsets, band_weights):
@@ -487,7 +514,7 @@
     slabs, gains = lax.switch(
         branch[0], [functools.partial(move, cap) for cap in CAPS], plan, raw_counts, dark_field, flat_field
     )
-    return rebin(plan, slabs, gains, band_offsets, band_weights)
+    return rebin(slabs, gains, band_offsets, band_weights)
 
 
 def solution(mesh):

time: 114 us -> 101 us (0.89)
  Pallas kernels: 112 us -> 99.1 us
    pallas_call x1, Pallas kernels: 17.3 us -> 11 us  [rebin(): pl.pallas_call(rebin_kernel, grid=(NDET // 2,), out_shape=jax.ShapeDtypeS...]
    pallas_call x1, Pallas kernels: 92.6 us -> 86.4 us  [move(): pl.pallas_call(functools.partial(move_kernel, cap), out_shape=(jax.ShapeD...]
where the time goes in v3:
time: 101 us; the launch traced here: 100 us
  Pallas kernels  99.1 us (98%)
    pallas_call x1, Pallas kernels, move(): pl.pallas_call(functools.partial(move_kernel, cap), out_shape=(jax.ShapeD...  86.4 us
    pallas_call x1, Pallas kernels, rebin(): pl.pallas_call(rebin_kernel, grid=(NDET // 2,), out_shape=jax.ShapeDtypeS...  11 us

profile of v3, /device:TPU:0, one launch (start us, length us, event | category | flops | bytes accessed | tf_op | source)
XLA Modules:
  0.0 100.2 jit_solution(15830097613958587054)
XLA Ops:
  0.0 1.7 %plan.1 = (s32[192]{0:T(256)S(1)}, s32[1]{0:T(128)}) custom-call(s32[32]{0:T(128)} %bitcast.4), custom_call_target="tpu_custom_call" | custom-call | tf_op jit(solution)/shard_map/plan/pallas_call | solution.py:63
  2.4 86.7 %conditional.1 = ((f32[16,2,4,8,8,256]{5,4,3,2,1,0:T(8,128)}, f32[2,16,8,256]{3,2,1,0:T(8,128)S(1)})) conditional(s32[]{:T(128)} %bitcast.1, (s32[192]{0:T(256)S(1)}, f32[32,128,256]{2,1,0:T(8,128)}, f32[128,256]{1,0:T(8,128)}, f32[128,256]{1,0:T(8,128)}) %tuple.17, (s32[192]{0:T(256)S(1)}, ...), branch_computations={%region_0.0_spmd, %region_1.0_spmd, %region_2.0_spmd, %region_3.0_... | conditional | bytes 8 | solution.py:514
  2.4 86.4 %move9.1 = (f32[16,2,4,8,8,256]{5,4,3,2,1,0:T(8,128)}, f32[2,16,8,256]{3,2,1,0:T(8,128)S(1)}) custom-call(s32[192]{0:T(256)S(1)} %get-tuple-element.37.plan, f32[32,128,256]{2,1,0:T(8,128)} %get-tuple-element.38.raw_hbm, f32[128,256]{1,0:T(8,128)} %get-tuple-element.39.dark, f32[128,256]{1,0:T(8,128)} %get-tuple-element.40.flat), custom_call_target="tpu_custom_call" | custom-call | tf_op jit(solution)/shard_map/cond/branch_0_fun/move9/pallas_call | solution.py:382
  89.0 11.0 %rebin.1 = f32[32,4,4,4096]{3,2,1,0:T(4,128)} custom-call(f32[16,2,4,8,8,256]{5,4,3,2,1,0:T(8,128)} %get-tuple-element.59.slabs_hbm, f32[2,16,8,256]{3,2,1,0:T(8,128)S(1)} %get-tuple-element.60.gains, s32[1,4096]{1,0:T(1,128)} %bitcast.3, f32[4,4096]{1,0:T(4,128)} %weights.1), custom_call_target="tpu_custom_call" | custom-call | tf_op jit(solution)/shard_map/rebin/pallas_call | solution.py:491
